TPU v7x, 256 devices: a whole 4x4x8 slice. The times are simulated.
256 devices in a mesh: seq: 32 (over z, x_hi, core), tp: 8 (over x_lo, y).
Axes of the slice: x: 4 (x_hi: 2, x_lo: 2; x = x_hi * 2 + x_lo), y: 4, z: 8, core: 2. Of those that a mesh axis runs over, the one named last changes fastest.
Arguments:
- query: bfloat16 [8192, 3584], P('seq', 'tp'), may hold values from -6 to 6
- keys: bfloat16 [8192, 3584], P('seq', 'tp'), may hold values from -6 to 6
- values: bfloat16 [8192, 3584], P('seq', 'tp'), may hold values from -6 to 6
- prefix_keys: bfloat16 [4096, 3584], P('seq', 'tp'), may hold values from -6 to 6
- prefix_values: bfloat16 [4096, 3584], P('seq', 'tp'), may hold values from -6 to 6
- residual: bfloat16 [8192, 3584], P('seq', 'tp'), may hold values from -4 to 4
- out_weight: bfloat16 [3584, 3584], P('tp'), may hold values from -1 to 1
- suffix_lens: int32 [16], replicated, may hold values from 1 to 2048, 8192 in all
- req_group: int32 [16], replicated, may hold values from 0 to 3
- placement: int32 [8192], replicated, may hold values from 0 to 8191, each once
- prefix_owner: int32 [32], replicated, may hold values from 0 to 3, as said below
Outputs:
- hidden: bfloat16 [8192, 3584], P('seq', 'tp')
- cache_keys: bfloat16 [8192, 3584], P('seq', 'tp')
- cache_values: bfloat16 [8192, 3584], P('seq', 'tp')
Inputs may be any that keep to these rules, and one draw needn't show every extreme that they name: `prefix_owner`: each group number appears exactly 8 times.
All inputs are finite; a program needn't handle non-finite values.
Results may differ from a plain program's by a relative error of at most 0.014.
Values may be sent and summed in bfloat16 or wider, within the bound.
A program may use at most 128 MiB of HBM per device.

v0:
```python
import math
import jax
import jax.numpy as jnp
from jax import lax
from jax.sharding import PartitionSpec as P

HD = 224
NEG_FILL = -1e30


def request_of(positions, ends):
    return jnp.sum((positions[:, None] >= ends[None, :]).astype(jnp.int32), axis=1)


def lookup_small(indices, table):
    slots = jnp.arange(table.shape[0], dtype=jnp.int32)
    return jnp.sum(jnp.where(indices[:, None] == slots[None, :], table[None, :], 0), axis=1)


def absorb(state, query_heads, key_piece, value_piece, visible):
    top, total, accum = state
    count = key_piece.shape[0]
    heads = query_heads.shape[1]
    head_size = query_heads.shape[2]
    key_heads = key_piece.reshape(count, heads, head_size)
    value_heads = value_piece.reshape(count, heads, head_size)
    scores = jnp.einsum(
        "qhd,khd->hqk", query_heads, key_heads, preferred_element_type=jnp.float32
    ) * (1.0 / math.sqrt(head_size))
    scores = jnp.where(visible[None], scores, NEG_FILL)
    fresh = jnp.maximum(top, jnp.max(scores, axis=2))
    weights = jnp.where(visible[None], jnp.exp(scores - fresh[:, :, None]), 0.0).astype(
        jnp.bfloat16
    )
    factor = jnp.exp(top - fresh)
    total = factor * total + jnp.sum(weights.astype(jnp.float32), axis=2)
    accum = factor[:, :, None] * accum + jnp.einsum(
        "hqk,khd->hqd", weights, value_heads, preferred_element_type=jnp.float32
    )
    return (fresh, total, accum)


def shards(
    query,
    keys,
    values,
    prefix_keys,
    prefix_values,
    residual,
    out_weight,
    suffix_lens,
    req_group,
    placement,
    prefix_owner,
):
    rows, width = query.shape
    block_rows = prefix_keys.shape[0]
    heads = width // HD
    me = lax.axis_index("seq")
    ends = jnp.cumsum(suffix_lens)
    my_pos = lax.dynamic_slice_in_dim(placement, me * rows, rows)
    my_req = request_of(my_pos, ends)
    my_grp = lookup_small(my_req, req_group)
    query_heads = query.reshape(rows, heads, HD)
    start_state = (
        jnp.full((heads, rows), NEG_FILL, jnp.float32),
        jnp.zeros((heads, rows), jnp.float32),
        jnp.zeros((heads, rows, HD), jnp.float32),
    )
    empty_cache = jnp.zeros((rows, width), jnp.bfloat16)
    pieces = (
        lax.all_gather(keys, "seq", axis=0, tiled=True),
        lax.all_gather(values, "seq", axis=0, tiled=True),
    )
    state = start_state
    cache = (empty_cache, empty_cache)
    count = pieces[0].shape[0]
    valid = jnp.ones((count,), jnp.bool_)
    key_req = request_of(placement, ends)
    state = absorb(
        state,
        query_heads,
        pieces[0],
        pieces[1],
        valid[None, :]
        & (key_req[None, :] == my_req[:, None])
        & (placement[None, :] <= my_pos[:, None]),
    )
    local = placement - me * rows
    keep = valid & (local >= 0) & (local < rows)
    target = jnp.where(keep, local, rows)
    cache = (
        cache[0].at[target].set(pieces[0], mode="drop"),
        cache[1].at[target].set(pieces[1], mode="drop"),
    )
    state, cache = (state, cache)
    pieces = (
        lax.all_gather(prefix_keys, "seq", axis=0, tiled=True),
        lax.all_gather(prefix_values, "seq", axis=0, tiled=True),
    )
    count = pieces[0].shape[0]
    key_block = jnp.arange(count, dtype=jnp.int32) // block_rows
    valid = jnp.ones((count,), jnp.bool_)
    key_grp = lookup_small(key_block, prefix_owner)
    state = absorb(
        state,
        query_heads,
        pieces[0],
        pieces[1],
        valid[None, :] & (key_grp[None, :] == my_grp[:, None]),
    )
    top, total, accum = state
    attended = accum / total[:, :, None]
    attended = jnp.transpose(attended, (1, 0, 2)).reshape(rows, width).astype(jnp.bfloat16)
    term = jnp.dot(attended, out_weight, preferred_element_type=jnp.float32)
    summed = lax.psum_scatter(
        term.astype(jnp.bfloat16), "tp", scatter_dimension=1, tiled=True
    ).astype(jnp.float32)
    hidden = (residual.astype(jnp.float32) + summed).astype(jnp.bfloat16)
    return (hidden, cache[0], cache[1])


def solution(mesh):
    return jax.shard_map(
        shards,
        mesh=mesh,
        in_specs=(
            P("seq", "tp"),
            P("seq", "tp"),
            P("seq", "tp"),
            P("seq", "tp"),
            P("seq", "tp"),
            P("seq", "tp"),
            P("tp", None),
            P(),
            P(),
            P(),
            P(),
        ),
        out_specs=(P("seq", "tp"), P("seq", "tp"), P("seq", "tp")),
        check_vma=False,
    )
```

profile of v0, /device:TPU:1, one launch (start us, length us, event | category | flops | bytes accessed | tf_op | source)
XLA Modules:
  0.0 508.1 jit_solution(1577933013104015989)
XLA Ops:
  7.2 0.7 all-gather.7.cloned.1.call-update
  8.0 0.7 all-gather.5.cloned.1.call-update
  8.7 0.7 all-gather.11.cloned.1.call-update
  9.4 0.5 all-gather.9.cloned.1.call-update
  10.0 0.0 reduce-scatter.2.cloned.1.call-start
  10.0 0.7 copy.20
  10.8 0.1 reduce
  10.9 0.8 dynamic_slice.3
  11.7 0.1 convert_reduce_fusion.3
  11.8 0.7 select_reduce_fusion.1
  12.5 0.9 convert_reduce_fusion.2
  13.4 0.8 select_reduce_fusion
  14.3 1.6 broadcast_compare_fusion
  15.9 3.6 compare_and_fusion
  19.4 79.9 %all-gather.7.cloned.1.call-done = bf16[4096,448]{0,1:T(8,128)(2,1)} async-done(((bf16[128,448]{0,1:T(8,128)(2,1)}), bf16[4096,448]{0,1:T(8,128)(2,1)}) %all-gather.7.cloned.1.call-update) | async-done | bytes 3670032 | tf_op jit(solution)/shard_map/all_gather | solution.py:98
  99.3 7.9 %fusion.1 = (f32[2,256]{1,0:T(2,128)S(1)}, f32[2,256,4096]{2,1,0:T(8,128)}) fusion(pred[256,4096]{1,0:T(8,128)(4,1)} %broadcast_compare_fusion, bf16[256,2,224]{0,2,1:T(8,128)(2,1)} %bitcast.56, bf16[4096,2,224]{0,2,1:T(8,128)(2,1)} %bitcast.55), kind=kOutput, calls=%fused_computation.10 | convolution fusion | flops 945815040 | bytes 13338624 | tf_op jit(solution)/shard_map/qhd,khd->hqk/dot_general | solution.py:27
  107.2 94.4 %all-gather.5.cloned.1.call-done = bf16[8192,448]{0,1:T(8,128)(2,1)} async-done(((bf16[256,448]{0,1:T(8,128)(2,1)}), bf16[8192,448]{0,1:T(8,128)(2,1)}) %all-gather.5.cloned.1.call-update) | async-done | bytes 7340048 | tf_op jit(solution)/shard_map/all_gather | solution.py:72
  201.6 12.2 %fusion = (f32[2,256]{1,0:T(2,128)S(1)}, f32[2,256,8192]{2,1,0:T(8,128)}) fusion(pred[256,8192]{1,0:T(8,128)(4,1)} %compare_and_fusion, bf16[256,2,224]{0,2,1:T(8,128)(2,1)S(1)} %bitcast.57, bf16[8192,2,224]{0,2,1:T(8,128)(2,1)} %bitcast.50), kind=kOutput, calls=%fused_computation.5 | convolution fusion | flops 1891630592 | bytes 26445824 | tf_op jit(solution)/shard_map/qhd,khd->hqk/dot_general | solution.py:27
  213.9 2.7 convert_reduce_fusion.1
  216.5 8.6 %convert_reduce_fusion = f32[2,256]{1,0:T(2,128)S(1)} fusion(f32[2,256]{1,0:T(2,128)S(1)} %get-tuple-element.12, f32[2,256,8192]{2,1,0:T(8,128)} %get-tuple-element.15, pred[256,8192]{1,0:T(8,128)(4,1)S(1)} %copy-done.1), kind=kLoop, calls=%fused_computation.2 | loop fusion | flops 29359616 | bytes 18878464 | tf_op jit(solution)/shard_map/reduce_sum | solution.py:36
  225.1 59.9 %all-gather.11.cloned.1.call-done = bf16[4096,448]{0,1:T(8,128)(2,1)} async-done(((bf16[128,448]{0,1:T(8,128)(2,1)}), bf16[4096,448]{0,1:T(8,128)(2,1)}) %all-gather.11.cloned.1.call-update) | async-done | bytes 3670032 | tf_op jit(solution)/shard_map/all_gather | solution.py:99
  285.0 7.7 %convolution_bitcast_fusion = f32[256,2,224]{0,2,1:T(8,128)} fusion(bf16[4096,2,224]{0,2,1:T(8,128)(2,1)} %bitcast.54, f32[2,256,4096]{2,1,0:T(8,128)} %get-tuple-element.17, f32[2,256]{1,0:T(2,128)S(1)} %get-tuple-element.13, pred[256,4096]{1,0:T(8,128)(4,1)} %broadcast_compare_fusion), kind=kOutput, calls=%fused_computation.13 | convolution fusion | flops 950009856 | bytes 13568000 | tf_op jit(solution)/shard_map/hqk,khd->hqd/dot_general | solution.py:37
  292.8 94.4 %all-gather.9.cloned.1.call-done = bf16[8192,448]{0,1:T(8,128)(2,1)} async-done(((bf16[256,448]{0,1:T(8,128)(2,1)}), bf16[8192,448]{0,1:T(8,128)(2,1)}) %all-gather.9.cloned.1.call-update) | async-done | bytes 7340048 | tf_op jit(solution)/shard_map/all_gather | solution.py:73
  387.2 13.2 %fusion.6 = bf16[256,2,224]{0,2,1:T(8,128)(2,1)S(1)} fusion(f32[256,2,224]{0,2,1:T(8,128)} %convolution_bitcast_fusion, bf16[8192,2,224]{0,2,1:T(8,128)(2,1)} %bitcast.51, f32[256,2]{0,1:T(2,128)S(1)} %get-tuple-element.9, f32[256,2]{0,1:T(2,128)S(1)} %get-tuple-element.11, f32[256,2]{0,1:T(2,128)S(1)} %get-tuple-element.10, ...), kind=kOutput, calls=%fused_computation.19 | convolution fusion | flops 1900593152 | bytes 26910720 | tf_op jit(solution)/shard_map/hqk,khd->hqd/dot_general | solution.py:37
  400.4 2.9 convolution_convert_fusion
  403.3 11.6 %copy.21 = bf16[8192,448]{1,0:T(8,128)(2,1)} copy(bf16[8192,448]{0,1:T(8,128)(2,1)} %all-gather.5.cloned.1.call-done) | data formatting | bytes 14680064 | tf_op jit(solution)/shard_map/all_gather | solution.py:72
  414.9 35.8 %scatter_custom_fusion = bf16[256,448]{1,0:T(8,128)(2,1)S(1)} fusion(s32[8192]{0:T(1024)S(1)} %compare_select_fusion, bf16[8192,448]{1,0:T(8,128)(2,1)} %copy.21, bf16[]{:T(256)} %constant.47.clone.1), kind=kCustom, calls=%fused_computation.26 | custom fusion | bytes 229888 | tf_op jit(solution)/shard_map/scatter | solution.py:93
  450.7 0.8 copy.23
  451.5 11.6 %copy.22 = bf16[8192,448]{1,0:T(8,128)(2,1)} copy(bf16[8192,448]{0,1:T(8,128)(2,1)} %all-gather.9.cloned.1.call-done) | data formatting | bytes 14680064 | tf_op jit(solution)/shard_map/all_gather | solution.py:73
  463.1 35.8 %scatter_custom_fusion.1 = bf16[256,448]{1,0:T(8,128)(2,1)S(1)} fusion(s32[8192]{0:T(1024)S(1)} %compare_select_fusion, bf16[8192,448]{1,0:T(8,128)(2,1)} %copy.22, bf16[]{:T(256)} %constant.47.clone.1), kind=kCustom, calls=%fused_computation.24 | custom fusion | bytes 229888 | tf_op jit(solution)/shard_map/scatter | solution.py:94
  498.9 0.8 copy.24
  499.8 1.8 add_convert_fusion
  (23 shorter events, 0.3 us)
Async XLA Ops:
  7.2 393.2 %copy-start = (bf16[448,3584]{1,0:T(8,128)(2,1)S(1)}, bf16[448,3584]{1,0:T(8,128)(2,1)}, u32[]{:S(2)}) copy-start(bf16[448,3584]{1,0:T(8,128)(2,1)} %param.17) | copy-start | bytes 9633796
  7.2 92.1 %all-gather.7.cloned.1.call-start = ((), (), s32[]{:S(2)}) async-start(), calls=%async_computation.2 | async-start | bytes 3784704 | tf_op jit(solution)/shard_map/all_gather | solution.py:98
  7.9 193.7 %all-gather.5.cloned.1.call-start = ((), (), s32[]{:S(2)}) async-start(), calls=%async_computation.1 | async-start | bytes 7569408 | tf_op jit(solution)/shard_map/all_gather | solution.py:72
  8.7 276.4 %all-gather.11.cloned.1.call-start = ((), (), s32[]{:S(2)}) async-start(), calls=%async_computation.4 | async-start | bytes 3784704 | tf_op jit(solution)/shard_map/all_gather | solution.py:99
  9.4 377.8 %all-gather.9.cloned.1.call-start = ((), (), s32[]{:S(2)}) async-start(), calls=%async_computation.3 | async-start | bytes 7569408 | tf_op jit(solution)/shard_map/all_gather | solution.py:73
  10.0 489.8 %reduce-scatter.2.cloned.1.call-start = ((), (), s32[]{:S(2)}) async-start(), calls=%async_computation.5 | async-start | bytes 2064384 | tf_op jit(solution)/shard_map/reduce_scatter | solution.py:116
  19.4 182.1 %copy-start.5 = (bf16[256,448]{0,1:T(8,128)(2,1)S(1)}, bf16[256,448]{0,1:T(8,128)(2,1)}, u32[]{:S(2)}) copy-start(bf16[256,448]{0,1:T(8,128)(2,1)} %param.11) | copy-start | bytes 688132
  201.6 12.3 %copy-start.2 = (f32[2,256,4096]{2,1,0:T(8,128)S(1)}, f32[2,256,4096]{2,1,0:T(8,128)}, u32[]{:S(2)}) copy-start(f32[2,256,4096]{2,1,0:T(8,128)} %get-tuple-element.17) | copy-start | bytes 25165828
  201.6 12.3 %copy-start.3 = (pred[256,4096]{1,0:T(8,128)(4,1)S(1)}, pred[256,4096]{1,0:T(8,128)(4,1)}, u32[]{:S(2)}) copy-start(pred[256,4096]{1,0:T(8,128)(4,1)} %broadcast_compare_fusion) | copy-start | bytes 3145732
  213.8 2.7 copy-start.1
  387.2 16.1 %copy-start.4 = (s32[8192]{0:T(1024)S(1)}, s32[8192]{0:T(1024)}, u32[]{:S(2)}) copy-start(s32[8192]{0:T(1024)} %param.20) | copy-start | bytes 98308
Sparse Core Ops, SparseCore 0:
  10.6 88.6 all-gather.6
  101.8 99.6 all-gather.4
  204.1 80.8 all-gather.10
  287.5 99.6 all-gather.8
  403.4 35.0 reduce-scatter.1
where the time goes:
time: 509 us; the launch traced here: 508 us
  waiting for transfers between devices  331 us (65%)
  local copies, waits for them, and re-layouts  98 us (19%)
  matrix products  43.9 us (9%)
  other arithmetic  21 us (4%)
  between operations  13.9 us (3%)
    all_gather x1, waiting for transfers between devices, shards(): lax.all_gather(values, 'seq', axis=0, tiled=True)  94.4 us
    all_gather x1, waiting for transfers between devices, shards(): lax.all_gather(keys, 'seq', axis=0, tiled=True)  94.4 us
    all_gather x1, waiting for transfers between devices, shards(): lax.all_gather(prefix_keys, 'seq', axis=0, tiled=True)  79.9 us
    all_gather x1, waiting for transfers between devices, shards(): lax.all_gather(prefix_values, 'seq', axis=0, tiled=True)  59.9 us
    scatter x1, local copies, waits for them, and re-layouts, shards(): cache[0].at[target].set(pieces[0], mode='drop')  35.8 us
    scatter x1, local copies, waits for them, and re-layouts, shards(): cache[1].at[target].set(pieces[1], mode='drop')  35.8 us
    dot_general x2, matrix products, absorb(): jnp.einsum('hqk,khd->hqd', weights, value_heads, preferred_element_type=j...  20.9 us
    dot_general x2, matrix products, absorb(): jnp.einsum('qhd,khd->hqk', query_heads, key_heads, preferred_element_type...  20.1 us
  transfers between devices with their start and end apart: 5, of which 4 were waited for; matrix products, arithmetic and copies ran while one was open for 29% of the time, Pallas kernels for 0%

commit v1 on v0

--- a/solution.py
+++ b/solution.py
@@ -6,6 +6,13 @@
 
 HD = 224
 NEG_FILL = -1e30
+
+
+def swapped_in(block, axis, along):
+    size = lax.axis_size(axis)
+    blocks = jnp.stack([block for _ in range(size)])
+    blocks = lax.all_to_all(blocks, axis, split_axis=0, concat_axis=0)
+    return jnp.concatenate(blocks, axis=along)
 
 
 def request_of(positions, ends):
@@ -95,7 +102,7 @@
     )
     state, cache = (state, cache)
     pieces = (
-        lax.all_gather(prefix_keys, "seq", axis=0, tiled=True),
+        swapped_in(prefix_keys, "seq", 0),
         lax.all_gather(prefix_values, "seq", axis=0, tiled=True),
     )
     count = pieces[0].shape[0]

time: 509 us -> 467 us (0.917)
  waiting for transfers between devices: 331 us -> 264 us
  local copies, waits for them, and re-layouts: 98 us -> 113 us
  starting transfers between devices: 0.19 us -> 12.8 us
    all_to_all x0 -> x1, waiting for transfers between devices: none -> 90.2 us  [swapped_in(): blocks = lax.all_to_all(blocks, axis, split_axis=0, concat_axis=0)]
    all_gather x1 -> x0, waiting for transfers between devices: 79.9 us -> none  [shards(): lax.all_gather(prefix_keys, 'seq', axis=0, tiled=True)]
    all_gather x1, waiting for transfers between devices: 94.4 us -> 18 us  [shards(): lax.all_gather(keys, 'seq', axis=0, tiled=True)]
    all_to_all x0 -> x1, starting transfers between devices: none -> 12.6 us  [swapped_in(): blocks = lax.all_to_all(blocks, axis, split_axis=0, concat_axis=0)]
    another operation x1 -> x3, local copies, waits for them, and re-layouts: 0.73 us -> 10.3 us  [the longest x1 6.68 us: absorb(): key_heads = key_piece.reshape(count, heads, head_size)]
    all_to_all x0 -> x1, local copies, waits for them, and re-layouts: none -> 6.24 us  [swapped_in(): blocks = lax.all_to_all(blocks, axis, split_axis=0, concat_axis=0)]
  transfers between devices with their start and end apart: 5 -> 5, of which waited for: 4 -> 4; matrix products, arithmetic and copies ran while one was open for 29% -> 34% of each run, Pallas kernels for 0% -> 0%
where the time goes in v1:
time: 467 us; the launch traced here: 466 us
  waiting for transfers between devices  264 us (57%)
  local copies, waits for them, and re-layouts  113 us (24%)
  matrix products  43.9 us (9%)
  other arithmetic  18.4 us (4%)
  between operations  13.9 us (3%)
  starting transfers between devices  12.8 us (3%)
    all_gather x1, waiting for transfers between devices, shards(): lax.all_gather(values, 'seq', axis=0, tiled=True)  94.6 us
    all_to_all x1, waiting for transfers between devices, swapped_in(): blocks = lax.all_to_all(blocks, axis, split_axis=0, concat_axis=0)  90.2 us
    all_gather x1, waiting for transfers between devices, shards(): lax.all_gather(prefix_values, 'seq', axis=0, tiled=True)  58.9 us
    scatter x1, local copies, waits for them, and re-layouts, shards(): cache[0].at[target].set(pieces[0], mode='drop')  35.8 us
    scatter x1, local copies, waits for them, and re-layouts, shards(): cache[1].at[target].set(pieces[1], mode='drop')  35.8 us
    dot_general x2, matrix products, absorb(): jnp.einsum('hqk,khd->hqd', weights, value_heads, preferred_element_type=j...  20.9 us
    dot_general x2, matrix products, absorb(): jnp.einsum('qhd,khd->hqk', query_heads, key_heads, preferred_element_type...  20.2 us
    all_gather x1, waiting for transfers between devices, shards(): lax.all_gather(keys, 'seq', axis=0, tiled=True)  18 us
  transfers between devices with their start and end apart: 5, of which 4 were waited for; matrix products, arithmetic and copies ran while one was open for 34% of the time, Pallas kernels for 0%

profile of v1, /device:TPU:1, one launch (start us, length us, event | category | flops | bytes accessed | tf_op | source)
XLA Modules:
  0.0 465.9 jit_solution(42279962767189021)
XLA Ops:
  7.3 0.7 all-gather.4.cloned.1.call-update
  8.0 0.7 all-gather.8.cloned.1.call-update
  8.8 0.7 all-gather.6.cloned.1.call-update
  9.4 3.6 stack.2
  13.0 12.6 %all-to-all-start = ((bf16[32,128,448]{1,2,0:T(8,128)(2,1)}), bf16[32,128,448]{1,2,0:T(8,128)(2,1)}, u32[]{:S(2)}, u32[]{:S(2)}) async-start(bf16[32,128,448]{1,2,0:T(8,128)(2,1)} %stack.2), calls=%async_computation | async-start | bytes 7340032 | tf_op jit(solution)/shard_map/all_to_all | solution.py:14
  25.8 0.1 reduce
  26.0 0.1 convert_reduce_fusion.3
  26.1 0.1 select_reduce_fusion.1
  26.2 0.2 convert_reduce_fusion.2
  26.4 0.2 select_reduce_fusion
  26.6 1.6 broadcast_compare_fusion
  28.2 2.8 compare_and_fusion
  31.0 90.2 %all-to-all-done = bf16[32,128,448]{1,2,0:T(8,128)(2,1)} async-done(((bf16[32,128,448]{1,2,0:T(8,128)(2,1)}), bf16[32,128,448]{1,2,0:T(8,128)(2,1)}, u32[]{:S(2)}, u32[]{:S(2)}) %all-to-all-start) | async-done | bytes 3670048 | tf_op jit(solution)/shard_map/all_to_all | solution.py:14
  121.2 6.2 %copy.27 = bf16[32,128,448]{1,0,2:T(8,128)(2,1)} copy(bf16[32,128,448]{1,2,0:T(8,128)(2,1)} %all-to-all-done) | data formatting | bytes 7340032 | tf_op jit(solution)/shard_map/all_to_all | solution.py:14
  127.5 6.7 %reshape_reshape.3 = bf16[4096,2,224]{0,2,1:T(8,128)(2,1)} reshape(bf16[32,128,448]{1,0,2:T(8,128)(2,1)} %copy.27) | data formatting | bytes 7340032 | tf_op jit(solution)/shard_map/reshape;reshape | solution.py:32
  134.1 7.9 %fusion.1 = (f32[2,256]{1,0:T(2,128)S(1)}, f32[2,256,4096]{2,1,0:T(8,128)}) fusion(pred[256,4096]{1,0:T(8,128)(4,1)} %broadcast_compare_fusion, bf16[256,2,224]{0,2,1:T(8,128)(2,1)S(1)} %bitcast.56, bf16[4096,2,224]{0,2,1:T(8,128)(2,1)} %reshape_reshape.3), kind=kOutput, calls=%fused_computation.10 | convolution fusion | flops 945815040 | bytes 13338624 | tf_op jit(solution)/shard_map/qhd,khd->hqk/dot_general | solution.py:34
  142.1 18.0 %all-gather.4.cloned.1.call-done = bf16[8192,448]{0,1:T(8,128)(2,1)} async-done(((bf16[256,448]{0,1:T(8,128)(2,1)}), bf16[8192,448]{0,1:T(8,128)(2,1)}) %all-gather.4.cloned.1.call-update) | async-done | bytes 7340048 | tf_op jit(solution)/shard_map/all_gather | solution.py:79
  160.1 12.2 %fusion = (f32[2,256]{1,0:T(2,128)S(1)}, f32[2,256,8192]{2,1,0:T(8,128)}) fusion(pred[256,8192]{1,0:T(8,128)(4,1)} %compare_and_fusion, bf16[256,2,224]{0,2,1:T(8,128)(2,1)S(1)} %bitcast.57, bf16[8192,2,224]{0,2,1:T(8,128)(2,1)} %bitcast.51), kind=kOutput, calls=%fused_computation.5 | convolution fusion | flops 1891630592 | bytes 26445824 | tf_op jit(solution)/shard_map/qhd,khd->hqk/dot_general | solution.py:34
  172.4 2.7 convert_reduce_fusion.1
  175.0 8.8 %convert_reduce_fusion = f32[2,256]{1,0:T(2,128)S(1)} fusion(f32[2,256]{1,0:T(2,128)S(1)} %get-tuple-element.15, f32[2,256,8192]{2,1,0:T(8,128)} %get-tuple-element.18, pred[256,8192]{1,0:T(8,128)(4,1)S(1)} %copy-done.1), kind=kLoop, calls=%fused_computation.2 | loop fusion | flops 29359616 | bytes 18878464 | tf_op jit(solution)/shard_map/reduce_sum | solution.py:43
  183.9 58.9 %all-gather.8.cloned.1.call-done = bf16[4096,448]{0,1:T(8,128)(2,1)} async-done(((bf16[128,448]{0,1:T(8,128)(2,1)}), bf16[4096,448]{0,1:T(8,128)(2,1)}) %all-gather.8.cloned.1.call-update) | async-done | bytes 3670032 | tf_op jit(solution)/shard_map/all_gather | solution.py:106
  242.8 7.7 %convolution_bitcast_fusion = f32[256,2,224]{0,2,1:T(8,128)} fusion(bf16[4096,2,224]{0,2,1:T(8,128)(2,1)} %bitcast.55, f32[2,256,4096]{2,1,0:T(8,128)} %get-tuple-element.20, f32[2,256]{1,0:T(2,128)S(1)} %get-tuple-element.16, pred[256,4096]{1,0:T(8,128)(4,1)} %broadcast_compare_fusion), kind=kOutput, calls=%fused_computation.13 | convolution fusion | flops 950009856 | bytes 13568000 | tf_op jit(solution)/shard_map/hqk,khd->hqd/dot_general | solution.py:44
  250.5 94.6 %all-gather.6.cloned.1.call-done = bf16[8192,448]{0,1:T(8,128)(2,1)} async-done(((bf16[256,448]{0,1:T(8,128)(2,1)}), bf16[8192,448]{0,1:T(8,128)(2,1)}) %all-gather.6.cloned.1.call-update) | async-done | bytes 7340048 | tf_op jit(solution)/shard_map/all_gather | solution.py:80
  345.0 13.2 %fusion.6 = bf16[256,2,224]{0,2,1:T(8,128)(2,1)S(1)} fusion(f32[256,2,224]{0,2,1:T(8,128)} %convolution_bitcast_fusion, bf16[8192,2,224]{0,2,1:T(8,128)(2,1)} %bitcast.52, f32[256,2]{0,1:T(2,128)S(1)} %get-tuple-element.12, f32[256,2]{0,1:T(2,128)S(1)} %get-tuple-element.14, f32[256,2]{0,1:T(2,128)S(1)} %get-tuple-element.13, ...), kind=kOutput, calls=%fused_computation.19 | convolution fusion | flops 1900593152 | bytes 26910720 | tf_op jit(solution)/shard_map/hqk,khd->hqd/dot_general | solution.py:44
  358.2 2.9 convolution_convert_fusion
  361.1 11.6 %copy.28 = bf16[8192,448]{1,0:T(8,128)(2,1)} copy(bf16[8192,448]{0,1:T(8,128)(2,1)} %all-gather.4.cloned.1.call-done) | data formatting | bytes 14680064 | tf_op jit(solution)/shard_map/all_gather | solution.py:79
  372.7 35.8 %scatter_custom_fusion = bf16[256,448]{1,0:T(8,128)(2,1)S(1)} fusion(s32[8192]{0:T(1024)S(1)} %compare_select_fusion, bf16[8192,448]{1,0:T(8,128)(2,1)} %copy.28, bf16[]{:T(256)} %constant.47.clone.1), kind=kCustom, calls=%fused_computation.26 | custom fusion | bytes 229888 | tf_op jit(solution)/shard_map/scatter | solution.py:100
  408.6 0.8 copy.30
  409.4 11.6 %copy.29 = bf16[8192,448]{1,0:T(8,128)(2,1)} copy(bf16[8192,448]{0,1:T(8,128)(2,1)} %all-gather.6.cloned.1.call-done) | data formatting | bytes 14680064 | tf_op jit(solution)/shard_map/all_gather | solution.py:80
  421.0 35.8 %scatter_custom_fusion.1 = bf16[256,448]{1,0:T(8,128)(2,1)S(1)} fusion(s32[8192]{0:T(1024)S(1)} %compare_select_fusion, bf16[8192,448]{1,0:T(8,128)(2,1)} %copy.29, bf16[]{:T(256)} %constant.47.clone.1), kind=kCustom, calls=%fused_computation.24 | custom fusion | bytes 229888 | tf_op jit(solution)/shard_map/scatter | solution.py:101
  456.8 0.8 copy.31
  457.6 1.8 add_convert_fusion
  (31 shorter events, 0.5 us)
Async XLA Ops:
  7.2 351.1 %copy-start = (bf16[448,3584]{1,0:T(8,128)(2,1)S(1)}, bf16[448,3584]{1,0:T(8,128)(2,1)}, u32[]{:S(2)}) copy-start(bf16[448,3584]{1,0:T(8,128)(2,1)} %param.17) | copy-start | bytes 9633796
  7.2 18.5 %copy-start.6 = (s32[16]{0:T(128)S(1)}, s32[16]{0:T(128)}, u32[]{:S(2)}) copy-start(s32[16]{0:T(128)} %param.18) | copy-start | bytes 196
  7.2 18.8 %copy-start.4 = (s32[8192]{0:T(1024)S(1)}, s32[8192]{0:T(1024)}, u32[]{:S(2)}) copy-start(s32[8192]{0:T(1024)} %param.20) | copy-start | bytes 98308
  7.2 18.9 %copy-start.7 = (s32[16]{0:T(128)S(1)}, s32[16]{0:T(128)}, u32[]{:S(2)}) copy-start(s32[16]{0:T(128)} %param.19) | copy-start | bytes 196
  7.2 19.2 %copy-start.5 = (s32[32]{0:T(128)S(1)}, s32[32]{0:T(128)}, u32[]{:S(2)}) copy-start(s32[32]{0:T(128)} %param.21) | copy-start | bytes 388
  7.2 152.9 %all-gather.4.cloned.1.call-start = ((), (), s32[]{:S(2)}) async-start(), calls=%async_computation.2 | async-start | bytes 7569408 | tf_op jit(solution)/shard_map/all_gather | solution.py:79
  8.0 234.8 %all-gather.8.cloned.1.call-start = ((), (), s32[]{:S(2)}) async-start(), calls=%async_computation.4 | async-start | bytes 3784704 | tf_op jit(solution)/shard_map/all_gather | solution.py:106
  8.7 336.3 %all-gather.6.cloned.1.call-start = ((), (), s32[]{:S(2)}) async-start(), calls=%async_computation.3 | async-start | bytes 7569408 | tf_op jit(solution)/shard_map/all_gather | solution.py:80
  13.0 108.2 %all-to-all-start = ((bf16[32,128,448]{1,2,0:T(8,128)(2,1)}), bf16[32,128,448]{1,2,0:T(8,128)(2,1)}, u32[]{:S(2)}, u32[]{:S(2)}) async-start(bf16[32,128,448]{1,2,0:T(8,128)(2,1)} %stack.2), calls=%async_computation | async-start | bytes 7340032 | tf_op jit(solution)/shard_map/all_to_all | solution.py:14
  25.6 432.0 %reduce-scatter.2.cloned.1.call-start = ((), (), s32[]{:S(2)}) async-start(), calls=%async_computation.5 | async-start | bytes 2064384 | tf_op jit(solution)/shard_map/reduce_scatter | solution.py:123
  28.2 105.9 %copy-start.8 = (bf16[256,448]{0,1:T(8,128)(2,1)S(1)}, bf16[256,448]{0,1:T(8,128)(2,1)}, u32[]{:S(2)}) copy-start(bf16[256,448]{0,1:T(8,128)(2,1)} %param.11) | copy-start | bytes 688132
  160.1 12.3 %copy-start.2 = (f32[2,256,4096]{2,1,0:T(8,128)S(1)}, f32[2,256,4096]{2,1,0:T(8,128)}, u32[]{:S(2)}) copy-start(f32[2,256,4096]{2,1,0:T(8,128)} %get-tuple-element.20) | copy-start | bytes 25165828
  160.1 12.3 %copy-start.3 = (pred[256,4096]{1,0:T(8,128)(4,1)S(1)}, pred[256,4096]{1,0:T(8,128)(4,1)}, u32[]{:S(2)}) copy-start(pred[256,4096]{1,0:T(8,128)(4,1)} %broadcast_compare_fusion) | copy-start | bytes 3145732
  172.3 2.7 copy-start.1
Sparse Core Ops, SparseCore 0:
  10.6 149.4 all-gather.3
  162.6 80.0 all-gather.7
  245.3 99.6 all-gather.5
  361.2 35.0 reduce-scatter.1
